TPU v7x, 512 devices: a whole 4x4x16 slice. The times are simulated.
512 devices in a mesh: band: 16 (over z_hi, x, core), dom: 32 (over z_lo, y).
Axes of the slice: x: 4, y: 4, z: 16 (z_hi: 2, z_lo: 8; z = z_hi * 8 + z_lo), core: 2. Of those that a mesh axis runs over, the one named last changes fastest.
Arguments:
- orbitals: bfloat16 [20, 32, 8, 8, 4096], P(None, 'dom', None, None, 'band'), may hold values from -6 to 6
- rotation: bfloat16 [4096, 4096], P(None, 'band'), may hold values from -0.09375 to 0.09375
- potential: float32 [8, 32, 8, 8], P(None, 'dom'), may hold values from -4 to 4
Outputs:
- filtered: float32 [8, 32, 8, 8, 4096], P(None, 'dom', None, None, 'band')
All inputs are finite; a program needn't handle non-finite values.
Results may differ from a plain program's by a relative error of at most 0.0003.
Values may be sent and summed in bfloat16 or wider, within the bound.
No kernel may reach another device: no remote copies, remote signals or barrier semaphores. Data moves between devices by JAX's collectives and lax.ppermute only.
A program may use at most 64 MiB of HBM per device.

v0:
```python
import jax
import jax.numpy as jnp
from jax import lax
from jax.experimental import pallas as pl
from jax.experimental.pallas import tpu as pltpu
from jax.sharding import PartitionSpec as P

TILES_Y = 4


stencil_weights = (
    -5369.0 / 1800.0,
    12.0 / 7.0,
    -15.0 / 56.0,
    10.0 / 189.0,
    -1.0 / 112.0,
    2.0 / 1925.0,
    -1.0 / 16632.0,
)
inverse_spacing = 4.0
centre_shift = 20.0
spread_scale = 24.0

HALVES = 2
SIDE = 8
TAIL = 8
KERNEL_VMEM = 12 * 1024 * 1024

side_groups = [[h * SIDE + i for i in range(SIDE)] for h in range(HALVES)]
half_swap = [(b, (b + SIDE) % (HALVES * SIDE)) for b in range(HALVES * SIDE)]


def from_behind(value, axis, steps):
    count = lax.axis_size(axis)
    initial, last = (max(0, -steps), min(count, count - steps))
    return lax.ppermute(value, axis, [(source, source + steps) for source in range(initial, last)])


def along_y(value, steps):
    count = lax.axis_size("dom")
    pairs = [
        (source, source + steps)
        for source in range(count)
        if 0 <= source % TILES_Y + steps < TILES_Y
    ]
    return lax.ppermute(value, "dom", pairs)


def ramp(shape, axis):
    column = lax.broadcasted_iota(jnp.int32, shape, axis)
    return ((column * 159) & 255).astype(jnp.float32) / 256.0


def lateral_weights(extent, sources, place):
    factor = -0.5 * inverse_spacing / spread_scale
    shape = (extent * extent, sources)
    row = lax.broadcasted_iota(jnp.int32, shape, 0)
    first, second = place(lax.broadcasted_iota(jnp.int32, shape, 1))
    first = jnp.abs(row // extent - first)
    second = jnp.abs(row % extent - second)
    apart = jnp.where((first == 0) != (second == 0), first + second, 0)
    weights = jnp.zeros(shape, jnp.float32)
    for offset in range(1, len(stencil_weights)):
        weights = jnp.where(apart == offset, factor * stencil_weights[offset], weights)
    return weights


def store_terms(out_ref, matrix):
    rows = matrix.shape[0]
    for term in range(3):
        part = matrix.astype(jnp.bfloat16)
        out_ref[term * rows : (term + 1) * rows] = part
        matrix = matrix - part.astype(jnp.float32)


def along_planes(slab_ref, potential_ref, out_ref, first_ref, second_ref):
    reach = len(stencil_weights) - 1
    factor = -0.5 * inverse_spacing / spread_scale
    planes, points, columns = out_ref.shape
    extent = potential_ref.shape[1]
    cube = (planes * points // extent, extent, extent)
    across = lax.broadcasted_iota(jnp.int32, cube, 1) == lax.broadcasted_iota(jnp.int32, cube, 2)
    shift = jnp.where(across, jnp.broadcast_to(potential_ref[...][:, None, :], cube), 0.0)
    shift = jnp.sum(shift, axis=2, keepdims=True).reshape(planes, points, 1)
    shift = (shift - centre_shift) / spread_scale + 3.0 * factor * stencil_weights[0]
    width = 128
    for lane in range(0, columns, width):
        part = pl.ds(lane, width)
        for plane in range(planes):
            centre = slab_ref[plane + reach, :, part].astype(jnp.float32)
            total = shift[plane] * centre
            for offset in range(1, reach + 1):
                pair = slab_ref[plane + reach + offset, :, part].astype(jnp.float32)
                pair = pair + slab_ref[plane + reach - offset, :, part].astype(jnp.float32)
                total = total + factor * stencil_weights[offset] * pair
            out_ref[plane, :, part] = total
    halo = reach * extent

    def with_first(number):
        at = number // extent
        at = jnp.where(number >= points, at - extent - reach, at)
        at = jnp.where(number >= points + halo, at + extent, at)
        return at, number % extent

    def with_second(number):
        at = number % points
        return at // extent, at % extent + jnp.where(number < points, -extent, extent)

    store_terms(first_ref, lateral_weights(extent, first_ref.shape[1], with_first))
    store_terms(second_ref, lateral_weights(extent, second_ref.shape[1], with_second))


def lateral(
    partial_ref,
    middle_ref,
    below_first_ref,
    above_first_ref,
    below_second_ref,
    above_second_ref,
    first_ref,
    second_ref,
    out_ref,
):
    planes, points, columns = partial_ref.shape
    halo = above_first_ref.shape[1]
    largest = jnp.zeros((points, columns), jnp.float32)
    for plane in range(planes):
        here = jnp.concatenate(
            [middle_ref[plane], below_first_ref[plane, points - halo :], above_first_ref[plane]],
            axis=0,
        )
        there = jnp.concatenate([below_second_ref[plane], above_second_ref[plane]], axis=0)
        terms = jnp.dot(first_ref[...], here, preferred_element_type=jnp.float32)
        terms = terms + jnp.dot(second_ref[...], there, preferred_element_type=jnp.float32)
        total = partial_ref[plane] + (
            terms[:points] + (terms[points : 2 * points] + terms[2 * points :])
        )
        out_ref[plane * points : (plane + 1) * points] = total
        largest = jnp.maximum(largest, jnp.abs(total))
    largest = jnp.max(jnp.max(largest, axis=0, keepdims=True), axis=1, keepdims=True)
    largest = jnp.broadcast_to(largest, (TAIL, columns))
    exponent = jnp.floor(jnp.log2(jnp.maximum(largest, 2.0**-100))) - 13.0
    factor = jnp.exp2(ramp((TAIL, columns), 1) - exponent)[:1]
    for plane in range(planes):
        block = slice(plane * points, (plane + 1) * points)
        out_ref[block] = out_ref[block] * factor
    out_ref[planes * points :] = exponent


def filtered_code(slab, potential):
    reach = len(stencil_weights) - 1
    planes, extent_first, extent_second = potential.shape
    points, columns = slab.shape[1:]
    middle = slab[reach : reach + planes]
    below_second = along_y(middle, 1)
    above_second = along_y(middle, -1)
    below_first = from_behind(middle, "dom", TILES_Y)
    above_first = from_behind(middle[:, : reach * extent_second], "dom", -TILES_Y)
    vmem = pl.BlockSpec(memory_space=pltpu.VMEM)
    params = pltpu.CompilerParams(vmem_limit_bytes=KERNEL_VMEM)
    halo = reach * extent_second
    values = planes * points * columns
    partial, first, second = pl.pallas_call(
        along_planes,
        out_shape=(
            jax.ShapeDtypeStruct((planes, points, columns), jnp.float32),
            jax.ShapeDtypeStruct((3 * points, points + 2 * halo), jnp.bfloat16),
            jax.ShapeDtypeStruct((3 * points, 2 * points), jnp.bfloat16),
        ),
        in_specs=[vmem] * 2,
        out_specs=(vmem,) * 3,
        cost_estimate=pl.CostEstimate(
            flops=30 * values, bytes_accessed=2 * slab.size + 4 * values, transcendentals=0
        ),
        compiler_params=params,
        name="along_planes",
    )(slab, potential.reshape(planes * extent_first, extent_second))
    scaled = pl.pallas_call(
        lateral,
        out_shape=jax.ShapeDtypeStruct((planes * points + TAIL, columns), jnp.float32),
        in_specs=[vmem] * 8,
        out_specs=vmem,
        cost_estimate=pl.CostEstimate(
            flops=2 * planes * (first.size + second.size) * columns,
            bytes_accessed=16 * values,
            transcendentals=0,
        ),
        compiler_params=params,
        name="lateral",
    )(partial, middle, below_first, above_first, below_second, above_second, first, second)
    return scaled.astype(jnp.float16)


def spread(code):
    return lax.all_gather(code, "band", axis=0, axis_index_groups=side_groups)


def product(codes, matrix, rows, start=None):
    exponent = codes[:, rows : rows + 1].astype(jnp.float32)
    factor = jnp.exp2(exponent - ramp((1, 1, codes.shape[2]), 2))
    value = codes[:, :rows].astype(jnp.float32) * factor
    high = lax.reduce_precision(value, 8, 7)
    low = (value - high).astype(jnp.bfloat16)
    high = high.astype(jnp.bfloat16)
    dims = (((0, 2), (0, 1)), ((), ()))
    first = lax.dot_general(high, matrix, dims, preferred_element_type=jnp.float32)
    second = lax.dot_general(low, matrix, dims, preferred_element_type=jnp.float32)
    return (first if start is None else start + first) + second


def on_device(orbitals, rotation, potential):
    ghosted = orbitals.shape[0]
    extent_first = orbitals.shape[2]
    extent_second = orbitals.shape[3]
    columns = orbitals.shape[4]
    planes = potential.shape[0]
    new_columns = rotation.shape[1]
    rows = planes * extent_first * extent_second
    slab_local = orbitals.reshape(ghosted, extent_first * extent_second, columns)
    potential_local = potential.reshape(planes, extent_first, extent_second)

    code = filtered_code(slab_local, potential_local)
    rotation, code = lax.optimization_barrier((rotation, code))
    half = lax.axis_index("band") // SIDE
    halves = rotation.reshape(HALVES, SIDE, columns, new_columns)
    arrived = lax.ppermute(code, "band", half_swap)
    gathered = spread(code)
    own_matrix = lax.dynamic_index_in_dim(halves, half, 0, keepdims=False)
    own = product(gathered, own_matrix, rows)
    arrived, own = lax.optimization_barrier((arrived, own))
    gathered = spread(arrived)
    other_matrix = lax.dynamic_index_in_dim(halves, 1 - half, 0, keepdims=False)
    result = product(gathered, other_matrix, rows, own)
    return result.reshape(planes, 1, extent_first, extent_second, new_columns)


def solution(mesh):
    in_specs = (P(None, "dom", None, None, "band"), P(None, "band"), P(None, "dom", None, None))
    out_specs = P(None, "dom", None, None, "band")
    return jax.shard_map(
        on_device, mesh=mesh, in_specs=in_specs, out_specs=out_specs, check_vma=False
    )
```

profile of v0, /device:TPU:105, one launch (start us, length us, event | category | flops | bytes accessed | tf_op | source)
XLA Modules:
  0.0 74.9 jit_solution(8123212596783038311)
XLA Ops:
  0.0 0.0 copy-start
  0.0 1.1 %slice_bitcast_fusion.middle_ref = bf16[8,64,256]{2,1,0:T(8,128)(2,1)S(1)} fusion(bf16[20,1,8,8,256]{4,3,2,1,0:T(8,128)(2,1)} %param.3), kind=kLoop, calls=%fused_computation.34 | loop fusion | bytes 524288 | tf_op jit(solution)/shard_map/slice | solution.py:154
  1.1 2.1 %collective-permute-start.3 = (bf16[8,64,256]{2,1,0:T(8,128)(2,1)S(1)}, bf16[8,64,256]{2,1,0:T(8,128)(2,1)S(1)}, u32[]{:S(2)}, u32[]{:S(2)}) collective-permute-start(bf16[8,64,256]{2,1,0:T(8,128)(2,1)S(1)} %slice_bitcast_fusion.middle_ref), channel_id=1, source_target_pairs={{1,0},{2,1},{3,2},{5,4},{6,5},{7,6},{9,8},{10,9},{11,10},{13,12},{... | collective-permute-start | bytes 786440 | tf_op jit(solution)/shard_map/ppermute | solution.py:46
  3.2 3.2 %collective-permute-start.2 = (bf16[8,64,256]{2,1,0:T(8,128)(2,1)S(1)}, bf16[8,64,256]{2,1,0:T(8,128)(2,1)S(1)}, u32[]{:S(2)}, u32[]{:S(2)}) collective-permute-start(bf16[8,64,256]{2,1,0:T(8,128)(2,1)S(1)} %slice_bitcast_fusion.middle_ref), channel_id=1, source_target_pairs={{0,1},{1,2},{2,3},{4,5},{5,6},{6,7},{8,9},{9,10},{10,11},{12,13},{... | collective-permute-start | bytes 786440 | tf_op jit(solution)/shard_map/ppermute | solution.py:46
  6.4 4.8 %collective-permute-start = (bf16[8,64,256]{2,1,0:T(8,128)(2,1)S(1)}, bf16[8,64,256]{2,1,0:T(8,128)(2,1)S(1)}, u32[]{:S(2)}, u32[]{:S(2)}) collective-permute-start(bf16[8,64,256]{2,1,0:T(8,128)(2,1)S(1)} %slice_bitcast_fusion.middle_ref), channel_id=1, source_target_pairs={{0,4},{1,5},{2,6},{3,7},{4,8},{5,9},{6,10},{7,11},{8,12},{9,13},{1... | collective-permute-start | bytes 786440 | tf_op jit(solution)/shard_map/ppermute | solution.py:36
  11.2 1.9 %collective-permute-start.1 = (bf16[8,48,256]{2,1,0:T(8,128)(2,1)S(1)}, bf16[8,48,256]{2,1,0:T(8,128)(2,1)S(1)}, u32[]{:S(2)}, u32[]{:S(2)}) collective-permute-start(bf16[8,48,256]{2,1,0:T(8,128)(2,1)S(1)} %slice.28), channel_id=1, source_target_pairs={{4,0},{5,1},{6,2},{7,3},{8,4},{9,5},{10,6},{11,7},{12,8},{13,9},{1... | collective-permute-start | bytes 589832 | tf_op jit(solution)/shard_map/ppermute | solution.py:36
  13.2 0.0 copy-start.1
  13.2 1.1 %copy-done.1 = bf16[20,1,8,8,256]{4,3,2,1,0:T(8,128)(2,1)S(1)} copy-done((bf16[20,1,8,8,256]{4,3,2,1,0:T(8,128)(2,1)S(1)}, bf16[20,1,8,8,256]{4,3,2,1,0:T(8,128)(2,1)}, u32[]{:S(2)}) %copy-start.1) | copy-done | bytes 655384
  14.3 0.0 copy-start.2
  14.3 0.8 %copy-done.2 = f32[8,1,8,8]{3,2,1,0:T(8,128)S(1)} copy-done((f32[8,1,8,8]{3,2,1,0:T(8,128)S(1)}, f32[8,1,8,8]{3,2,1,0:T(8,128)}, u32[]{:S(2)}) %copy-start.2) | copy-done | bytes 2072
  15.0 0.7 along_planes.1
  15.7 3.5 %collective-permute-done.1.above_first_ref = bf16[8,48,256]{2,1,0:T(8,128)(2,1)S(1)} collective-permute-done((bf16[8,48,256]{2,1,0:T(8,128)(2,1)S(1)}, bf16[8,48,256]{2,1,0:T(8,128)(2,1)S(1)}, u32[]{:S(2)}, u32[]{:S(2)}) %collective-permute-start.1) | collective-permute-done | bytes 196640 | tf_op jit(solution)/shard_map/ppermute | solution.py:36
  19.3 0.0 collective-permute-done.3.above_second_ref
  19.3 0.0 collective-permute-done.2.below_second_ref
  19.3 0.0 collective-permute-done.below_first_ref
  19.3 0.7 lateral.1
  20.0 10.6 %collective-permute-start.4 = (f16[520,256]{1,0:T(8,128)(2,1)S(1)}, f16[520,256]{1,0:T(8,128)(2,1)S(1)}, u32[]{:S(2)}, u32[]{:S(2)}) collective-permute-start(f16[520,256]{1,0:T(8,128)(2,1)S(1)} %convert_element_type.38), channel_id=1, source_target_pairs={{0,256},{32,288},{64,320},{96,352},{128,384},{160,416},{192,448},{... | collective-permute-start | bytes 798728 | tf_op jit(solution)/shard_map/ppermute | solution.py:226
  30.7 19.3 %all-gather.4 = f16[4160,256]{1,0:T(8,128)(2,1)S(1)} all-gather(f16[520,256]{1,0:T(8,128)(2,1)S(1)} %convert_element_type.38), channel_id=2, replica_groups={{0,32,64,96,128,160,192,224},{256,288,320,352,384,416,448,480},{1,33,65..., dimensions={0}, use_global_device_ids=true | all-gather | bytes 2396160 | tf_op jit(solution)/shard_map/all_gather | solution.py:195
  50.0 0.0 copy-done
  50.0 0.7 fusion.17
  50.7 0.8 %fusion.24 = f32[512,256]{1,0:T(8,128)S(1)} fusion(f32[512,256]{1,0:T(8,128)S(1)} %fusion.17, f32[8,256]{1,0:T(8,128)S(1)} %exponential_bitcast_fusion.1, f16[8,520,256]{2,1,0:T(8,128)(2,1)S(1)} %bitcast.45, bf16[2,8,256,256]{3,2,1,0:T(8,128)(2,1)S(1)} %bitcast.37, s32[]{:T(128)S(6)} %select_n.13), kind=kOutput, calls=%fused_computation.24 | convolution fusion | flops 542244864 | bytes 4202500 | tf_op jit(solution)/shard_map/dot_general | solution.py:207
  51.5 0.0 collective-permute-done.4
  51.5 20.9 %all-gather.5 = f16[4160,256]{1,0:T(8,128)(2,1)S(1)} all-gather(f16[520,256]{1,0:T(8,128)(2,1)S(1)} %collective-permute-done.4), channel_id=3, replica_groups={{0,32,64,96,128,160,192,224},{256,288,320,352,384,416,448,480},{1,33,65..., dimensions={0}, use_global_device_ids=true | all-gather | bytes 2396160 | tf_op jit(solution)/shard_map/all_gather | solution.py:195
  72.4 0.8 %fusion.21 = f32[512,256]{1,0:T(8,128)S(1)} fusion(f32[8,256]{1,0:T(8,128)S(1)} %exponential_bitcast_fusion, f16[8,520,256]{2,1,0:T(8,128)(2,1)S(1)} %bitcast.41, bf16[2,8,256,256]{3,2,1,0:T(8,128)(2,1)S(1)} %bitcast.36, s32[]{:T(128)S(6)} %select_n.14), kind=kOutput, calls=%fused_computation.23 | convolution fusion | flops 542113792 | bytes 3678212 | tf_op jit(solution)/shard_map/dot_general | solution.py:207
  73.2 0.7 fusion.16
  74.0 0.9 %add_add_fusion = f32[512,256]{1,0:T(8,128)} fusion(f32[512,256]{1,0:T(8,128)S(1)} %fusion.21, f32[512,256]{1,0:T(8,128)S(1)} %fusion.24, f32[512,256]{1,0:T(8,128)S(1)} %fusion.16), kind=kLoop, calls=%fused_computation.33 | loop fusion | flops 262144 | bytes 2097152 | tf_op jit(solution)/shard_map/add | solution.py:208
  (7 shorter events, 0.1 us)
Async XLA Ops:
  0.0 50.0 %copy-start = (bf16[4096,256]{1,0:T(8,128)(2,1)S(1)}, bf16[4096,256]{1,0:T(8,128)(2,1)}, u32[]{:S(2)}) copy-start(bf16[4096,256]{1,0:T(8,128)(2,1)} %param.4) | copy-start | bytes 6291460
  1.1 18.1 %collective-permute-start.3 = (bf16[8,64,256]{2,1,0:T(8,128)(2,1)S(1)}, bf16[8,64,256]{2,1,0:T(8,128)(2,1)S(1)}, u32[]{:S(2)}, u32[]{:S(2)}) collective-permute-start(bf16[8,64,256]{2,1,0:T(8,128)(2,1)S(1)} %slice_bitcast_fusion.middle_ref), channel_id=1, source_target_pairs={{1,0},{2,1},{3,2},{5,4},{6,5},{7,6},{9,8},{10,9},{11,10},{13,12},{... | collective-permute-start | bytes 786440 | tf_op jit(solution)/shard_map/ppermute | solution.py:46
  3.2 16.1 %collective-permute-start.2 = (bf16[8,64,256]{2,1,0:T(8,128)(2,1)S(1)}, bf16[8,64,256]{2,1,0:T(8,128)(2,1)S(1)}, u32[]{:S(2)}, u32[]{:S(2)}) collective-permute-start(bf16[8,64,256]{2,1,0:T(8,128)(2,1)S(1)} %slice_bitcast_fusion.middle_ref), channel_id=1, source_target_pairs={{0,1},{1,2},{2,3},{4,5},{5,6},{6,7},{8,9},{9,10},{10,11},{12,13},{... | collective-permute-start | bytes 786440 | tf_op jit(solution)/shard_map/ppermute | solution.py:46
  6.4 12.8 %collective-permute-start = (bf16[8,64,256]{2,1,0:T(8,128)(2,1)S(1)}, bf16[8,64,256]{2,1,0:T(8,128)(2,1)S(1)}, u32[]{:S(2)}, u32[]{:S(2)}) collective-permute-start(bf16[8,64,256]{2,1,0:T(8,128)(2,1)S(1)} %slice_bitcast_fusion.middle_ref), channel_id=1, source_target_pairs={{0,4},{1,5},{2,6},{3,7},{4,8},{5,9},{6,10},{7,11},{8,12},{9,13},{1... | collective-permute-start | bytes 786440 | tf_op jit(solution)/shard_map/ppermute | solution.py:36
  11.2 8.0 %collective-permute-start.1 = (bf16[8,48,256]{2,1,0:T(8,128)(2,1)S(1)}, bf16[8,48,256]{2,1,0:T(8,128)(2,1)S(1)}, u32[]{:S(2)}, u32[]{:S(2)}) collective-permute-start(bf16[8,48,256]{2,1,0:T(8,128)(2,1)S(1)} %slice.28), channel_id=1, source_target_pairs={{4,0},{5,1},{6,2},{7,3},{8,4},{9,5},{10,6},{11,7},{12,8},{13,9},{1... | collective-permute-start | bytes 589832 | tf_op jit(solution)/shard_map/ppermute | solution.py:36
  13.2 1.1 %copy-start.1 = (bf16[20,1,8,8,256]{4,3,2,1,0:T(8,128)(2,1)S(1)}, bf16[20,1,8,8,256]{4,3,2,1,0:T(8,128)(2,1)}, u32[]{:S(2)}) copy-start(bf16[20,1,8,8,256]{4,3,2,1,0:T(8,128)(2,1)} %param.3) | copy-start | bytes 1966084
  14.3 0.8 %copy-start.2 = (f32[8,1,8,8]{3,2,1,0:T(8,128)S(1)}, f32[8,1,8,8]{3,2,1,0:T(8,128)}, u32[]{:S(2)}) copy-start(f32[8,1,8,8]{3,2,1,0:T(8,128)} %param.5) | copy-start | bytes 6148
  20.0 31.5 %collective-permute-start.4 = (f16[520,256]{1,0:T(8,128)(2,1)S(1)}, f16[520,256]{1,0:T(8,128)(2,1)S(1)}, u32[]{:S(2)}, u32[]{:S(2)}) collective-permute-start(f16[520,256]{1,0:T(8,128)(2,1)S(1)} %convert_element_type.38), channel_id=1, source_target_pairs={{0,256},{32,288},{64,320},{96,352},{128,384},{160,416},{192,448},{... | collective-permute-start | bytes 798728 | tf_op jit(solution)/shard_map/ppermute | solution.py:226
where the time goes:
time: 75.2 us; the launch traced here: 74.9 us
  blocking collectives  40.2 us (53%)
  starting transfers between devices  22.6 us (30%)
  waiting for transfers between devices  3.53 us (5%)
  matrix products  3.03 us (4%)
  local copies, waits for them, and re-layouts  3 us (4%)
  Pallas kernels  1.4 us (2%)
  other arithmetic  0.96 us (1%)
    all_gather x2, blocking collectives, spread(): return lax.all_gather(code, 'band', axis=0, axis_index_groups=side_groups)  40.2 us
    ppermute x1, starting transfers between devices, on_device(): arrived = lax.ppermute(code, 'band', half_swap)  10.6 us
    ppermute x2, starting transfers between devices, from_behind(): lax.ppermute(value, axis, [(source, source + steps) for source in range(i...  6.68 us
    ppermute x2, starting transfers between devices, along_y(): return lax.ppermute(value, 'dom', pairs)  5.28 us
    ppermute x2, waiting for transfers between devices, from_behind(): lax.ppermute(value, axis, [(source, source + steps) for source in range(i...  3.52 us
    unnamed x6, local copies, waits for them, and re-layouts  1.84 us
    dot_general x2, matrix products, product(): lax.dot_general(low, matrix, dims, preferred_element_type=jnp.float32)  1.59 us
  transfers between devices with their start and end apart: 5, of which 1 were waited for; matrix products, arithmetic and copies ran while one was open for 2% of the time, Pallas kernels for 1%

commit v1 on v0

--- a/solution.py
+++ b/solution.py
@@ -122,12 +122,10 @@
     out_ref,
 ):
     planes, points, columns = partial_ref.shape
-    halo = above_first_ref.shape[1]
     largest = jnp.zeros((points, columns), jnp.float32)
     for plane in range(planes):
         here = jnp.concatenate(
-            [middle_ref[plane], below_first_ref[plane, points - halo :], above_first_ref[plane]],
-            axis=0,
+            [middle_ref[plane], below_first_ref[plane], above_first_ref[plane]], axis=0
         )
         there = jnp.concatenate([below_second_ref[plane], above_second_ref[plane]], axis=0)
         terms = jnp.dot(first_ref[...], here, preferred_element_type=jnp.float32)
@@ -154,7 +152,7 @@
     middle = slab[reach : reach + planes]
     below_second = along_y(middle, 1)
     above_second = along_y(middle, -1)
-    below_first = from_behind(middle, "dom", TILES_Y)
+    below_first = from_behind(middle[:, (extent_first - reach) * extent_second :], "dom", TILES_Y)
     above_first = from_behind(middle[:, : reach * extent_second], "dom", -TILES_Y)
     vmem = pl.BlockSpec(memory_space=pltpu.VMEM)
     params = pltpu.CompilerParams(vmem_limit_bytes=KERNEL_VMEM)

time: 75.2 us -> 75.4 us (level)
  the two profiles are of different devices: /device:TPU:105 before, /device:TPU:33 now
where the time goes in v1:
time: 75.4 us; the launch traced here: 75.1 us
  blocking collectives  36.9 us (49%)
  starting transfers between devices  26.1 us (35%)
  local copies, waits for them, and re-layouts  3.69 us (5%)
  matrix products  3.02 us (4%)
  waiting for transfers between devices  2.79 us (4%)
  Pallas kernels  1.41 us (2%)
  other arithmetic  0.96 us (1%)
    all_gather x2, blocking collectives, spread(): return lax.all_gather(code, 'band', axis=0, axis_index_groups=side_groups)  36.9 us
    ppermute x1, starting transfers between devices, on_device(): arrived = lax.ppermute(code, 'band', half_swap)  15.4 us
    ppermute x2, starting transfers between devices, from_behind(): lax.ppermute(value, axis, [(source, source + steps) for source in range(i...  5.45 us
    ppermute x2, starting transfers between devices, along_y(): return lax.ppermute(value, 'dom', pairs)  5.29 us
    ppermute x1, waiting for transfers between devices, on_device(): arrived = lax.ppermute(code, 'band', half_swap)  2.24 us
    unnamed x6, local copies, waits for them, and re-layouts  1.84 us
    dot_general x2, matrix products, product(): lax.dot_general(low, matrix, dims, preferred_element_type=jnp.float32)  1.58 us
  transfers between devices with their start and end apart: 5, of which 2 were waited for; matrix products, arithmetic and copies ran while one was open for 3% of the time, Pallas kernels for 1%

profile of v1, /device:TPU:33, one launch (start us, length us, event | category | flops | bytes accessed | tf_op | source)
XLA Modules:
  0.0 75.1 jit_solution(5647558328088930973)
XLA Ops:
  0.0 0.0 copy-start
  0.0 1.1 %slice_bitcast_fusion.middle_ref = bf16[8,64,256]{2,1,0:T(8,128)(2,1)S(1)} fusion(bf16[20,1,8,8,256]{4,3,2,1,0:T(8,128)(2,1)} %param.3), kind=kLoop, calls=%fused_computation.34 | loop fusion | bytes 524288 | tf_op jit(solution)/shard_map/slice | solution.py:152
  1.1 1.3 %collective-permute-start.3 = (bf16[8,64,256]{2,1,0:T(8,128)(2,1)S(1)}, bf16[8,64,256]{2,1,0:T(8,128)(2,1)S(1)}, u32[]{:S(2)}, u32[]{:S(2)}) collective-permute-start(bf16[8,64,256]{2,1,0:T(8,128)(2,1)S(1)} %slice_bitcast_fusion.middle_ref), channel_id=1, source_target_pairs={{1,0},{2,1},{3,2},{5,4},{6,5},{7,6},{9,8},{10,9},{11,10},{13,12},{... | collective-permute-start | bytes 786440 | tf_op jit(solution)/shard_map/ppermute | solution.py:46
  2.4 4.0 %collective-permute-start.2 = (bf16[8,64,256]{2,1,0:T(8,128)(2,1)S(1)}, bf16[8,64,256]{2,1,0:T(8,128)(2,1)S(1)}, u32[]{:S(2)}, u32[]{:S(2)}) collective-permute-start(bf16[8,64,256]{2,1,0:T(8,128)(2,1)S(1)} %slice_bitcast_fusion.middle_ref), channel_id=1, source_target_pairs={{0,1},{1,2},{2,3},{4,5},{5,6},{6,7},{8,9},{9,10},{10,11},{12,13},{... | collective-permute-start | bytes 786440 | tf_op jit(solution)/shard_map/ppermute | solution.py:46
  6.4 0.7 fusion.39
  7.1 1.9 %collective-permute-start.1 = (bf16[8,48,256]{2,1,0:T(8,128)(2,1)}, bf16[8,48,256]{2,1,0:T(8,128)(2,1)S(1)}, u32[]{:S(2)}, u32[]{:S(2)}) collective-permute-start(bf16[8,48,256]{2,1,0:T(8,128)(2,1)} %get-tuple-element.19), channel_id=1, source_target_pairs={{4,0},{5,1},{6,2},{7,3},{8,4},{9,5},{10,6},{11,7},{12,8},{13,9},{1... | collective-permute-start | bytes 589832 | tf_op jit(solution)/shard_map/ppermute | solution.py:36
  9.1 3.5 %collective-permute-start = (bf16[8,48,256]{2,1,0:T(8,128)(2,1)S(1)}, bf16[8,48,256]{2,1,0:T(8,128)(2,1)S(1)}, u32[]{:S(2)}, u32[]{:S(2)}) collective-permute-start(bf16[8,48,256]{2,1,0:T(8,128)(2,1)S(1)} %get-tuple-element.20), channel_id=1, source_target_pairs={{0,4},{1,5},{2,6},{3,7},{4,8},{5,9},{6,10},{7,11},{8,12},{9,13},{1... | collective-permute-start | bytes 589832 | tf_op jit(solution)/shard_map/ppermute | solution.py:36
  12.6 0.0 copy-start.1
  12.6 1.1 %copy-done.1 = bf16[20,1,8,8,256]{4,3,2,1,0:T(8,128)(2,1)S(1)} copy-done((bf16[20,1,8,8,256]{4,3,2,1,0:T(8,128)(2,1)S(1)}, bf16[20,1,8,8,256]{4,3,2,1,0:T(8,128)(2,1)}, u32[]{:S(2)}) %copy-start.1) | copy-done | bytes 655384
  13.7 0.0 copy-start.2
  13.7 0.8 %copy-done.2 = f32[8,1,8,8]{3,2,1,0:T(8,128)S(1)} copy-done((f32[8,1,8,8]{3,2,1,0:T(8,128)S(1)}, f32[8,1,8,8]{3,2,1,0:T(8,128)}, u32[]{:S(2)}) %copy-start.2) | copy-done | bytes 2072
  14.5 0.7 along_planes.1
  15.2 0.0 collective-permute-done.1.above_first_ref
  15.2 0.5 collective-permute-done.below_first_ref
  15.8 0.0 collective-permute-done.3.above_second_ref
  15.8 0.0 collective-permute-done.2.below_second_ref
  15.8 0.7 lateral.1
  16.5 15.4 %collective-permute-start.4 = (f16[520,256]{1,0:T(8,128)(2,1)S(1)}, f16[520,256]{1,0:T(8,128)(2,1)S(1)}, u32[]{:S(2)}, u32[]{:S(2)}) collective-permute-start(f16[520,256]{1,0:T(8,128)(2,1)S(1)} %convert_element_type.38), channel_id=1, source_target_pairs={{0,256},{32,288},{64,320},{96,352},{128,384},{160,416},{192,448},{... | collective-permute-start | bytes 798728 | tf_op jit(solution)/shard_map/ppermute | solution.py:224
  31.9 19.3 %all-gather.4 = f16[4160,256]{1,0:T(8,128)(2,1)S(1)} all-gather(f16[520,256]{1,0:T(8,128)(2,1)S(1)} %convert_element_type.38), channel_id=2, replica_groups={{0,32,64,96,128,160,192,224},{256,288,320,352,384,416,448,480},{1,33,65..., dimensions={0}, use_global_device_ids=true | all-gather | bytes 2396160 | tf_op jit(solution)/shard_map/all_gather | solution.py:193
  51.2 0.0 copy-done
  51.2 0.7 fusion.17
  52.0 0.8 %fusion.24 = f32[512,256]{1,0:T(8,128)S(1)} fusion(f32[512,256]{1,0:T(8,128)S(1)} %fusion.17, f32[8,256]{1,0:T(8,128)S(1)} %exponential_bitcast_fusion.1, f16[8,520,256]{2,1,0:T(8,128)(2,1)S(1)} %bitcast.45, bf16[2,8,256,256]{3,2,1,0:T(8,128)(2,1)S(1)} %bitcast.37, s32[]{:T(128)S(6)} %select_n.13), kind=kOutput, calls=%fused_computation.24 | convolution fusion | flops 542244864 | bytes 4202500 | tf_op jit(solution)/shard_map/dot_general | solution.py:205
  52.8 2.2 %collective-permute-done.4 = f16[520,256]{1,0:T(8,128)(2,1)S(1)} collective-permute-done((f16[520,256]{1,0:T(8,128)(2,1)S(1)}, f16[520,256]{1,0:T(8,128)(2,1)S(1)}, u32[]{:S(2)}, u32[]{:S(2)}) %collective-permute-start.4) | collective-permute-done | bytes 266272 | tf_op jit(solution)/shard_map/ppermute | solution.py:224
  55.0 17.6 %all-gather.5 = f16[4160,256]{1,0:T(8,128)(2,1)S(1)} all-gather(f16[520,256]{1,0:T(8,128)(2,1)S(1)} %collective-permute-done.4), channel_id=3, replica_groups={{0,32,64,96,128,160,192,224},{256,288,320,352,384,416,448,480},{1,33,65..., dimensions={0}, use_global_device_ids=true | all-gather | bytes 2396160 | tf_op jit(solution)/shard_map/all_gather | solution.py:193
  72.7 0.8 %fusion.21 = f32[512,256]{1,0:T(8,128)S(1)} fusion(f32[8,256]{1,0:T(8,128)S(1)} %exponential_bitcast_fusion, f16[8,520,256]{2,1,0:T(8,128)(2,1)S(1)} %bitcast.41, bf16[2,8,256,256]{3,2,1,0:T(8,128)(2,1)S(1)} %bitcast.36, s32[]{:T(128)S(6)} %select_n.14), kind=kOutput, calls=%fused_computation.23 | convolution fusion | flops 542113792 | bytes 3678212 | tf_op jit(solution)/shard_map/dot_general | solution.py:205
  73.5 0.7 fusion.16
  74.2 0.9 %add_add_fusion = f32[512,256]{1,0:T(8,128)} fusion(f32[512,256]{1,0:T(8,128)S(1)} %fusion.21, f32[512,256]{1,0:T(8,128)S(1)} %fusion.24, f32[512,256]{1,0:T(8,128)S(1)} %fusion.16), kind=kLoop, calls=%fused_computation.33 | loop fusion | flops 262144 | bytes 2097152 | tf_op jit(solution)/shard_map/add | solution.py:206
  (6 shorter events, 0.1 us)
Async XLA Ops:
  0.0 51.2 %copy-start = (bf16[4096,256]{1,0:T(8,128)(2,1)S(1)}, bf16[4096,256]{1,0:T(8,128)(2,1)}, u32[]{:S(2)}) copy-start(bf16[4096,256]{1,0:T(8,128)(2,1)} %param.4) | copy-start | bytes 6291460
  1.1 14.6 %collective-permute-start.3 = (bf16[8,64,256]{2,1,0:T(8,128)(2,1)S(1)}, bf16[8,64,256]{2,1,0:T(8,128)(2,1)S(1)}, u32[]{:S(2)}, u32[]{:S(2)}) collective-permute-start(bf16[8,64,256]{2,1,0:T(8,128)(2,1)S(1)} %slice_bitcast_fusion.middle_ref), channel_id=1, source_target_pairs={{1,0},{2,1},{3,2},{5,4},{6,5},{7,6},{9,8},{10,9},{11,10},{13,12},{... | collective-permute-start | bytes 786440 | tf_op jit(solution)/shard_map/ppermute | solution.py:46
  2.4 13.3 %collective-permute-start.2 = (bf16[8,64,256]{2,1,0:T(8,128)(2,1)S(1)}, bf16[8,64,256]{2,1,0:T(8,128)(2,1)S(1)}, u32[]{:S(2)}, u32[]{:S(2)}) collective-permute-start(bf16[8,64,256]{2,1,0:T(8,128)(2,1)S(1)} %slice_bitcast_fusion.middle_ref), channel_id=1, source_target_pairs={{0,1},{1,2},{2,3},{4,5},{5,6},{6,7},{8,9},{9,10},{10,11},{12,13},{... | collective-permute-start | bytes 786440 | tf_op jit(solution)/shard_map/ppermute | solution.py:46
  7.1 8.1 %collective-permute-start.1 = (bf16[8,48,256]{2,1,0:T(8,128)(2,1)}, bf16[8,48,256]{2,1,0:T(8,128)(2,1)S(1)}, u32[]{:S(2)}, u32[]{:S(2)}) collective-permute-start(bf16[8,48,256]{2,1,0:T(8,128)(2,1)} %get-tuple-element.19), channel_id=1, source_target_pairs={{4,0},{5,1},{6,2},{7,3},{8,4},{9,5},{10,6},{11,7},{12,8},{13,9},{1... | collective-permute-start | bytes 589832 | tf_op jit(solution)/shard_map/ppermute | solution.py:36
  9.1 6.7 %collective-permute-start = (bf16[8,48,256]{2,1,0:T(8,128)(2,1)S(1)}, bf16[8,48,256]{2,1,0:T(8,128)(2,1)S(1)}, u32[]{:S(2)}, u32[]{:S(2)}) collective-permute-start(bf16[8,48,256]{2,1,0:T(8,128)(2,1)S(1)} %get-tuple-element.20), channel_id=1, source_target_pairs={{0,4},{1,5},{2,6},{3,7},{4,8},{5,9},{6,10},{7,11},{8,12},{9,13},{1... | collective-permute-start | bytes 589832 | tf_op jit(solution)/shard_map/ppermute | solution.py:36
  12.6 1.1 %copy-start.1 = (bf16[20,1,8,8,256]{4,3,2,1,0:T(8,128)(2,1)S(1)}, bf16[20,1,8,8,256]{4,3,2,1,0:T(8,128)(2,1)}, u32[]{:S(2)}) copy-start(bf16[20,1,8,8,256]{4,3,2,1,0:T(8,128)(2,1)} %param.3) | copy-start | bytes 1966084
  13.7 0.8 %copy-start.2 = (f32[8,1,8,8]{3,2,1,0:T(8,128)S(1)}, f32[8,1,8,8]{3,2,1,0:T(8,128)}, u32[]{:S(2)}) copy-start(f32[8,1,8,8]{3,2,1,0:T(8,128)} %param.5) | copy-start | bytes 6148
  16.5 38.5 %collective-permute-start.4 = (f16[520,256]{1,0:T(8,128)(2,1)S(1)}, f16[520,256]{1,0:T(8,128)(2,1)S(1)}, u32[]{:S(2)}, u32[]{:S(2)}) collective-permute-start(f16[520,256]{1,0:T(8,128)(2,1)S(1)} %convert_element_type.38), channel_id=1, source_target_pairs={{0,256},{32,288},{64,320},{96,352},{128,384},{160,416},{192,448},{... | collective-permute-start | bytes 798728 | tf_op jit(solution)/shard_map/ppermute | solution.py:224
